TPU v7x, 32 devices: a whole 2x2x4 slice. The times are simulated.
32 devices in a mesh: expert: 4 (over y, core), dp: 2 (over x), tensor: 4 (over z).
Axes of the slice: x: 2, y: 2, z: 4, core: 2. Of those that a mesh axis runs over, the one named last changes fastest.
Arguments:
- tokens: bfloat16 [128, 4096], P(('expert', 'dp')), may hold values from -6 to 6
- expert_ids: int32 [128, 2], P(('expert', 'dp')), may hold values from 0 to 3, all different within a row; in each aligned block of 16 rows (0 to 15, 16 to 31, ...) at most 12 rows name the same one
- route_weight: float32 [128, 2], P(('expert', 'dp')), may hold values from 0.2 to 1
- gate_weight: bfloat16 [4, 4096, 8192], P('expert', None, ('dp', 'tensor')), may hold values from -0.09375 to 0.09375
- up_weight: bfloat16 [4, 4096, 8192], P('expert', None, ('dp', 'tensor')), may hold values from -0.09375 to 0.09375
- down_weight: bfloat16 [4, 8192, 4096], P('expert', 'dp', 'tensor'), may hold values from -0.125 to 0.125
- past_layers: bfloat16 [8, 128, 4096], P(None, ('expert', 'dp'), 'tensor'), may hold values from -6 to 6
- dwa_weight: float32 [9], replicated, may hold values from 0.3 to 1.2
Outputs:
- mixed: bfloat16 [128, 4096], P(('expert', 'dp'), 'tensor')
Inputs may be any that keep to these rules, and one draw needn't show every extreme that they name: `expert_ids`: each row names 2 different experts. In each aligned block of 16 rows (the rows of one device) no expert is named more than 12 times; in some blocks one expert is named exactly 12 times.
All inputs are finite; a program needn't handle non-finite values.
Results may differ from a plain program's by a relative error of at most 0.009.
Values may be sent and summed in bfloat16 or wider, within the bound.
A program may use at most 64 MiB of HBM per device.

v0:
```python
import jax
import jax.numpy as jnp
from jax import lax
from jax.sharding import PartitionSpec as P


def assignment_slots(expert_ids, experts, capacity):
    flat_ids = expert_ids.reshape(-1)
    matches = (flat_ids[:, None] == jnp.arange(experts, dtype=jnp.int32)[None, :]).astype(jnp.int32)
    earlier = jnp.cumsum(matches, axis=0) - matches
    slot_ids = jnp.sum(earlier * matches, axis=1)
    return flat_ids * capacity + slot_ids


def selector(expert_ids, experts, capacity):
    targets = assignment_slots(expert_ids, experts, capacity)
    matched = targets[None, :] == jnp.arange(experts * capacity, dtype=jnp.int32)[:, None]
    chosen = matched.reshape(experts * capacity, expert_ids.shape[0], expert_ids.shape[1])
    return jnp.sum(chosen.astype(jnp.float32), axis=2).astype(jnp.bfloat16)


def per_device(
    tokens, expert_ids, route_weight, gate_weight, up_weight, down_weight, past_layers, dwa_weight
):
    experts = lax.axis_size("expert")
    tok_rows, feature_width = tokens.shape
    chosen_count = expert_ids.shape[1]
    capacity = min(tok_rows, 3 * chosen_count * tok_rows // (2 * experts))
    w_gate = gate_weight[0]
    w_up = up_weight[0]
    w_down = down_weight[0]
    targets = assignment_slots(expert_ids, experts, capacity)
    selected = selector(expert_ids, experts, capacity)
    packed = jnp.dot(selected, tokens, preferred_element_type=jnp.float32).astype(jnp.bfloat16)
    packed = packed.reshape(experts, capacity, feature_width)
    arrived = lax.all_to_all(packed, "expert", split_axis=0, concat_axis=0, tiled=True)
    block_rows = lax.all_gather(
        arrived.reshape(experts * capacity, feature_width), "dp", axis=0, tiled=True
    )
    gate = jnp.dot(block_rows, w_gate, preferred_element_type=jnp.float32)
    up = jnp.dot(block_rows, w_up, preferred_element_type=jnp.float32)
    hidden = (jax.nn.silu(gate) * up).astype(jnp.bfloat16)
    hidden_wide = lax.all_gather(hidden, "tensor", axis=1, tiled=True)
    expert_out = lax.psum_scatter(
        jnp.dot(hidden_wide, w_down, preferred_element_type=jnp.float32),
        "dp",
        scatter_dimension=0,
        tiled=True,
    ).astype(jnp.bfloat16)
    quarter = expert_out.shape[1]
    returned_rows = lax.all_to_all(
        expert_out.reshape(experts, capacity, quarter),
        "expert",
        split_axis=0,
        concat_axis=0,
        tiled=True,
    )
    returned_rows = returned_rows.reshape(experts * capacity, quarter)
    fetched = returned_rows[targets].astype(jnp.float32).reshape(tok_rows, chosen_count, quarter)
    shares = route_weight / jnp.sum(route_weight, axis=1, keepdims=True)
    expert_mix = jnp.sum(fetched * shares[:, :, None], axis=1)
    first_column = lax.axis_index("tensor") * quarter
    residual = lax.dynamic_slice_in_dim(tokens, first_column, quarter, 1).astype(jnp.float32)
    current = residual + expert_mix
    depth = past_layers.shape[0]
    history = jnp.einsum("j,jtd->td", dwa_weight[:depth], past_layers.astype(jnp.float32))
    return (dwa_weight[depth] * current + history).astype(jnp.bfloat16)


def solution(mesh):
    return jax.shard_map(
        per_device,
        mesh=mesh,
        in_specs=(
            P(("expert", "dp"), None),
            P(("expert", "dp"), None),
            P(("expert", "dp"), None),
            P("expert", None, ("dp", "tensor")),
            P("expert", None, ("dp", "tensor")),
            P("expert", "dp", "tensor"),
            P(None, ("expert", "dp"), "tensor"),
            P(),
        ),
        out_specs=P(("expert", "dp"), "tensor"),
        check_vma=False,
    )
```

profile of v0, /device:TPU:0, one launch (start us, length us, event | category | flops | bytes accessed | tf_op | source)
XLA Modules:
  0.0 97.0 jit_solution(14708177083163517885)
XLA Ops:
  6.5 0.8 copy.15
  7.3 0.1 eq.15
  7.6 0.2 select_reduce_fusion
  8.0 1.2 %convolution_convert_fusion = bf16[48,4096]{1,0:T(8,128)(2,1)S(1)} fusion(bf16[16,4096]{1,0:T(8,128)(2,1)} %param.8, bf16[48,16]{0,1:T(8,128)(2,1)S(1)} %convert_reduce_fusion), kind=kOutput, calls=%fused_computation.7 | convolution fusion | flops 6488064 | bytes 525824 | tf_op jit(solution)/shard_map/dot_general | solution.py:34
  9.2 0.1 reshape.66
  9.3 12.9 %all_to_all.10 = bf16[4,12,4096]{2,1,0:T(8,128)(2,1)S(1)} all-to-all(bf16[4,12,4096]{2,1,0:T(8,128)(2,1)S(1)} %reshape.66), channel_id=1, replica_groups=mesh['expert'=4,'dp'=2,'tensor'=4] {'expert'}, dimensions={0} | all-to-all | bytes 786432 | tf_op jit(solution)/shard_map/all_to_all | solution.py:36
  22.2 0.1 reshape.67
  22.3 11.2 %all_gather.6 = bf16[96,4096]{1,0:T(8,128)(2,1)S(1)} all-gather(bf16[48,4096]{1,0:T(8,128)(2,1)S(1)} %reshape.67), channel_id=1, replica_groups=mesh['expert'=4,'dp'=2,'tensor'=4] {'dp'}, dimensions={0}, use_global_device_ids=true | all-gather | bytes 1179648 | tf_op jit(solution)/shard_map/all_gather | solution.py:37
  33.4 5.0 %fusion.4 = f32[96,1024]{1,0:T(8,128)S(1)} fusion(bf16[96,4096]{1,0:T(8,128)(2,1)S(1)} %all_gather.6, bf16[1,4096,1024]{2,1,0:T(8,128)(2,1)} %param.11), kind=kOutput, calls=%fused_computation.5 | convolution fusion | flops 805306368 | bytes 9568256 | tf_op jit(solution)/shard_map/dot_general | solution.py:40
  38.5 5.1 %fusion.9 = bf16[96,1024]{1,0:T(8,128)(2,1)S(1)} fusion(bf16[96,4096]{1,0:T(8,128)(2,1)S(1)} %all_gather.6, bf16[1,4096,1024]{2,1,0:T(8,128)(2,1)} %param.12, f32[96,1024]{1,0:T(8,128)S(1)} %fusion.4), kind=kOutput, calls=%fused_computation.9 | convolution fusion | flops 805896192 | bytes 9764864 | tf_op jit(solution)/shard_map/dot_general | solution.py:41
  43.5 19.6 %all_gather.7 = bf16[96,4096]{1,0:T(8,128)(2,1)S(1)} all-gather(bf16[96,1024]{1,0:T(8,128)(2,1)S(1)} %fusion.9), channel_id=1, replica_groups=mesh['expert'=4,'dp'=2,'tensor'=4] {'tensor'}, dimensions={1}, use_global_device_ids=true | all-gather | bytes 983040 | tf_op jit(solution)/shard_map/all_gather | solution.py:43
  63.1 2.2 %fusion = f32[96,1024]{1,0:T(8,128)} fusion(bf16[96,4096]{1,0:T(8,128)(2,1)S(1)} %all_gather.7, bf16[1,4096,1024]{2,1,0:T(8,128)(2,1)S(1)} %bitcast.33), kind=kOutput, calls=%fused_computation.1 | convolution fusion | flops 805306368 | bytes 9568256 | tf_op jit(solution)/shard_map/dot_general | solution.py:45
  65.5 0.1 copy.18
  65.6 0.6 slice.6
  66.2 0.3 fusion.12
  66.4 11.2 %reduce-scatter.2.cloned.1.call-done = f32[48,1024]{1,0:T(8,128)} async-done(((f32[96,1024]{1,0:T(8,128)}), f32[48,1024]{1,0:T(8,128)}) %reduce-scatter.2.cloned.1.call-update) | async-done | bytes 196624 | tf_op jit(solution)/shard_map/reduce_scatter | solution.py:44
  77.7 0.9 convert_element_type.39
  78.6 0.7 reshape.68
  79.3 3.3 %all-to-all-start.1 = ((bf16[4,12,1024]{2,1,0:T(8,128)(2,1)}), bf16[4,12,1024]{2,1,0:T(8,128)(2,1)S(1)}, u32[]{:S(2)}, u32[]{:S(2)}) async-start(bf16[4,12,1024]{2,1,0:T(8,128)(2,1)} %reshape.68), calls=%async_computation.2 | async-start | bytes 262144 | tf_op jit(solution)/shard_map/all_to_all | solution.py:51
  82.6 4.6 %all-to-all-done.1 = bf16[4,12,1024]{2,1,0:T(8,128)(2,1)S(1)} async-done(((bf16[4,12,1024]{2,1,0:T(8,128)(2,1)}), bf16[4,12,1024]{2,1,0:T(8,128)(2,1)S(1)}, u32[]{:S(2)}, u32[]{:S(2)}) %all-to-all-start.1) | async-done | bytes 98336 | tf_op jit(solution)/shard_map/all_to_all | solution.py:51
  87.2 0.6 gather_fusion
  87.8 0.1 reshape.70
  87.9 0.2 multiply_reduce_fusion
  88.2 2.0 %fusion.14 = bf16[16,1024]{1,0:T(8,128)(2,1)} fusion(f32[1,16,1024]{2,0,1:T(1,128)S(1)} %fusion.12, f32[16,1024]{1,0:T(8,128)S(1)} %multiply_reduce_fusion, bf16[16,4096]{1,0:T(8,128)(2,1)} %param.8, s32[]{:T(128)S(6)} %select_n.13, f32[]{:T(128)} %bitcast), kind=kLoop, calls=%fused_computation.14 | loop fusion | flops 81920 | bytes 196616 | tf_op jit(solution)/shard_map/convert_element_type | solution.py:67
  (25 shorter events, 0.6 us)
Async XLA Ops:
  6.5 59.6 %copy-start = (bf16[8,16,1024]{2,1,0:T(8,128)(2,1)S(1)}, bf16[8,16,1024]{2,1,0:T(8,128)(2,1)}, u32[]{:S(2)}) copy-start(bf16[8,16,1024]{2,1,0:T(8,128)(2,1)} %param.14) | copy-start | bytes 786436
  6.5 71.1 %reduce-scatter.2.cloned.1.call-start = ((), (), s32[]{:S(2)}) async-start(), calls=%async_computation.3 | async-start | bytes 589824 | tf_op jit(solution)/shard_map/reduce_scatter | solution.py:44
  33.4 29.6 %slice-start = ((s8[8388608]{0:T(1024)(128)(4,1)}), s8[4194304]{0:T(1024)(128)(4,1)S(1)}, s32[]{:S(2)}) async-start(s8[8388608]{0:T(1024)(128)(4,1)} %bitcast.32), calls=%async_computation.4 | async-start | bytes 8388608
  38.4 24.6 %slice-start.1 = ((s8[8388608]{0:T(1024)(128)(4,1)}), s8[4194304]{0:T(1024)(128)(4,1)S(1)}, s32[]{:S(2)}) async-start(s8[8388608]{0:T(1024)(128)(4,1)} %bitcast.32), calls=%async_computation.5 | async-start | bytes 8388608
  63.1 2.4 %copy-start.1 = (f32[16,2]{0,1:T(2,128)S(1)}, f32[16,2]{0,1:T(2,128)}, u32[]{:S(2)}) copy-start(f32[16,2]{0,1:T(2,128)} %param.10) | copy-start | bytes 388
  63.1 2.5 %copy-start.2 = (f32[9]{0:T(128)S(1)}, f32[9]{0:T(128)}, u32[]{:S(2)}) copy-start(f32[9]{0:T(128)} %param.15) | copy-start | bytes 112
  79.3 7.9 %all-to-all-start.1 = ((bf16[4,12,1024]{2,1,0:T(8,128)(2,1)}), bf16[4,12,1024]{2,1,0:T(8,128)(2,1)S(1)}, u32[]{:S(2)}, u32[]{:S(2)}) async-start(bf16[4,12,1024]{2,1,0:T(8,128)(2,1)} %reshape.68), calls=%async_computation.2 | async-start | bytes 262144 | tf_op jit(solution)/shard_map/all_to_all | solution.py:51
Sparse Core Ops, SparseCore 0:
  65.5 12.1 reduce-scatter.1
where the time goes:
time: 97.3 us; the launch traced here: 97 us
  blocking collectives  43.6 us (45%)
  waiting for transfers between devices  15.8 us (16%)
  matrix products  13.7 us (14%)
  between operations  13.5 us (14%)
  other arithmetic  3.56 us (4%)
  local copies, waits for them, and re-layouts  3.41 us (4%)
  starting transfers between devices  3.32 us (3%)
    all_gather x1, blocking collectives, per_device(): hidden_wide = lax.all_gather(hidden, 'tensor', axis=1, tiled=True)  19.6 us
    all_to_all x1, blocking collectives, per_device(): lax.all_to_all(packed, 'expert', split_axis=0, concat_axis=0, tiled=True)  12.9 us
    reduce_scatter x1, waiting for transfers between devices, per_device(): lax.psum_scatter(jnp.dot(hidden_wide, w_down, preferred_element_type=jnp....  11.2 us
    all_gather x1, blocking collectives, per_device(): lax.all_gather(arrived.reshape(experts * capacity, feature_width), 'dp',...  11.2 us
    dot_general x1, matrix products, per_device(): up = jnp.dot(block_rows, w_up, preferred_element_type=jnp.float32)  5.05 us
    dot_general x1, matrix products, per_device(): gate = jnp.dot(block_rows, w_gate, preferred_element_type=jnp.float32)  5 us
    all_to_all x1, waiting for transfers between devices, per_device(): lax.all_to_all(expert_out.reshape(experts, capacity, quarter), 'expert',...  4.55 us
    all_to_all x1, starting transfers between devices, per_device(): lax.all_to_all(expert_out.reshape(experts, capacity, quarter), 'expert',...  3.32 us
  transfers between devices with their start and end apart: 2, of which 2 were waited for; matrix products, arithmetic and copies ran while one was open for 1% of the time, Pallas kernels for 0%

commit v1 on v0

v1 whole, which is shorter than its diff:
```python
import functools

import jax
import jax.numpy as jnp
from jax import lax
from jax.experimental import pallas as pl
from jax.experimental.pallas import tpu as pltpu
from jax.sharding import PartitionSpec as P

MESH = pl.DeviceIdType.MESH
F32 = jnp.float32
BF16 = jnp.bfloat16


def arrival_order(n):
    table = []
    for z in range(n):
        order = [z]
        for k in range(1, n):
            order += [o for o in (z - k, z + k) if 0 <= o < n]
        table.append(order)
    return table


def kernel(
    sizes,
    tokens,
    ids,
    route,
    w_gate,
    w_up,
    w_down,
    past,
    dwa,
    out,
    rows_in,
    gate_buf,
    up_buf,
    down_buf,
    past_buf,
    hidden,
    acc,
    outgoing,
    incoming,
    base,
    local_sem,
    gate_sem,
    up_sem,
    down_sem,
    past_sem,
    tok_send,
    pair_send,
    tok_recv,
    z_send,
    z_recv,
    mix_send,
    mix_recv,
):
    n_exp, n_dp, n_ten, pieces, tok_rows, quarter = sizes
    columns = n_exp // 2
    in_group = 2 * n_dp
    e, d, z = (lax.axis_index(a) for a in ("expert", "dp", "tensor"))
    core = lax.rem(e, 2)
    col = lax.div(e, 2)
    partner = e + 1 - 2 * core
    piece = gate_buf.shape[2]

    def rows_at(position):
        return pl.ds(pl.multiple_of(position * tok_rows, tok_rows), tok_rows)

    loads = []
    own_place = core * n_dp + d
    own_load = pltpu.make_async_copy(tokens, rows_in.at[0, rows_at(own_place)], local_sem)
    own_load.start()
    for s in range(pieces):
        part = pl.ds(s * piece, piece)
        loads.append(
            (
                pltpu.make_async_copy(w_gate.at[0, :, part], gate_buf.at[s], gate_sem.at[s]),
                pltpu.make_async_copy(w_up.at[0, :, part], up_buf.at[s], up_sem.at[s]),
            )
        )
        for copy in loads[-1]:
            copy.start()
    past_load = pltpu.make_async_copy(past, past_buf, past_sem)
    past_load.start()
    table = arrival_order(n_ten)
    order = []
    for j in range(n_ten):
        o = jnp.int32(0)
        for i in range(n_ten):
            o = o + jnp.where(z == i, table[i][j], 0)
        order.append(o)
    depth = n_ten and down_buf.shape[1]
    down_loads = []
    for j in range(n_ten):
        o = order[j]
        down_loads.append(
            pltpu.make_async_copy(
                w_down.at[0, pl.ds(pl.multiple_of(o * depth, depth), depth)],
                down_buf.at[o],
                down_sem.at[o],
            )
        )
        down_loads[-1].start()

    barrier = pltpu.get_barrier_semaphore()
    peers = [(i, j) for i in range(n_exp) for j in range(n_dp) if (i, j) != (0, 0)]
    for i, j in peers:
        pl.semaphore_signal(
            barrier,
            inc=1,
            device_id=(lax.rem(e + i, n_exp), lax.rem(d + j, n_dp), z),
            device_id_type=MESH,
        )
    has_up = z < n_ten - 1
    has_down = z > 0
    if n_ten > 1:

        @pl.when(has_up)
        def _():
            pl.semaphore_signal(barrier, inc=1, device_id=(e, d, z + 1), device_id_type=MESH)

        @pl.when(has_down)
        def _():
            pl.semaphore_signal(barrier, inc=1, device_id=(e, d, z - 1), device_id_type=MESH)

    pl.semaphore_wait(barrier, len(peers) + has_up.astype(jnp.int32) + has_down.astype(jnp.int32))

    def to_partner(g, place, slot):
        source = tokens if slot == (0, 0) else rows_in.at[g, rows_at(place)]
        return pltpu.make_async_remote_copy(
            source,
            rows_in.at[g, rows_at(place)],
            pair_send.at[slot[0], slot[1]],
            tok_recv.at[g, place],
            device_id=(partner, d, z),
            device_id_type=MESH,
        )

    def direct(g, dd):
        return pltpu.make_async_remote_copy(
            tokens,
            rows_in.at[g, rows_at(own_place)],
            tok_send.at[g, dd],
            tok_recv.at[g, own_place],
            device_id=(
                2 * lax.rem(col + columns - g, columns) + core,
                lax.rem(d + dd, n_dp),
                z,
            ),
            device_id_type=MESH,
        )

    sends = [to_partner(0, own_place, (0, 0))]
    sends[0].start()
    hops = [(g, dd) for g in range(columns) for dd in range(n_dp) if (g, dd) != (0, 0)]
    for g, dd in sorted(hops, key=lambda h: (h[0] > 0) + (h[1] > 0)):
        copy = direct(g, dd)
        copy.start()
        sends.append(copy)

    def wait_tokens(g, place):
        pltpu.make_async_remote_copy(
            tokens,
            rows_in.at[g, rows_at(place)],
            tok_send.at[0, 0],
            tok_recv.at[g, place],
            device_id=(partner, d, z),
            device_id_type=MESH,
        ).wait_recv()

    def pass_on(g):
        for dd in range(n_dp):
            if (g, dd) == (0, 0):
                continue
            place = core * n_dp + lax.rem(d + n_dp - dd, n_dp)
            wait_tokens(g, place)
            copy = to_partner(g, place, (g, dd))
            copy.start()
            sends.append(copy)

    def from_partner(g):
        for dd in range(n_dp):
            wait_tokens(g, (1 - core) * n_dp + dd)

    def hop(g, o, s, up):
        return pltpu.make_async_remote_copy(
            hidden.at[g, o, s],
            hidden.at[g, o, s],
            z_send.at[g, o, s, 0 if up else 1],
            z_recv.at[g, o, s],
            device_id=(e, d, z + 1 if up else z - 1),
            device_id_type=MESH,
        )

    def first_half(g):
        for s in range(pieces):
            if g == 0:
                for copy in loads[s]:
                    copy.wait()
            rows = rows_in[g]
            gate = jnp.dot(rows, gate_buf[s], preferred_element_type=F32)
            up = jnp.dot(rows, up_buf[s], preferred_element_type=F32)
            hidden[g, z, s] = (gate / (1.0 + jnp.exp(-gate)) * up).astype(BF16)

            @pl.when(has_up)
            def _():
                hop(g, z, s, True).start()

            @pl.when(has_down)
            def _():
                hop(g, z, s, False).start()

    def relay(g, j):
        o = order[j]
        for s in range(pieces):
            hop(g, o, s, True).wait_recv()

            @pl.when((o < z) & has_up)
            def _():
                hop(g, o, s, True).start()

            @pl.when((o > z) & has_down)
            def _():
                hop(g, o, s, False).start()

    def second_half(g, j):
        o = order[j]
        total = None
        for s in range(pieces):
            term = jnp.dot(
                hidden[g, o, s],
                down_buf[o, pl.ds(s * piece, piece), :],
                preferred_element_type=F32,
            )
            total = term if total is None else total + term
        if j == 0:
            acc[g] = total
        else:
            acc[g] += total

    me = e * n_dp + d

    def give(g):
        outgoing[g] = acc[g].astype(BF16)
        copies = []
        for k in range(2):
            for dd in range(n_dp):
                place = lax.rem(core + k, 2) * n_dp + lax.rem(d + dd, n_dp)
                if (g, k, dd) == (0, 0, 0):
                    incoming[me] = outgoing[g, rows_at(place), :]
                    continue
                copy = pltpu.make_async_remote_copy(
                    outgoing.at[g, rows_at(place)],
                    incoming.at[me],
                    mix_send.at[g, k, dd],
                    mix_recv.at[me],
                    device_id=(
                        2 * lax.rem(col + g, columns) + lax.rem(core + k, 2),
                        lax.rem(d + dd, n_dp),
                        z,
                    ),
                    device_id_type=MESH,
                )
                copy.start()
                copies.append(copy)
        return copies

    past_load.wait()
    layers = past_buf.shape[0]
    history = dwa[0] * past_buf[0].astype(F32)
    for j in range(1, layers):
        history = history + dwa[j] * past_buf[j].astype(F32)
    base[...] = history
    own_load.wait()
    pass_on(0)
    from_partner(0)
    first_half(0)
    residual = rows_in[0, rows_at(own_place), pl.ds(pl.multiple_of(z * quarter, quarter), quarter)]
    base[...] += dwa[layers] * residual.astype(F32)
    for g in range(1, columns):
        pass_on(g)
        from_partner(g)
        first_half(g)
    mixes = []
    for j in range(n_ten):
        for g in range(columns):
            if j > 0:
                relay(g, j)
            if g == 0:
                down_loads[j].wait()
            second_half(g, j)
            if j == n_ten - 1:
                mixes += give(g)

    shares = route[...] / jnp.sum(route[...], axis=1, keepdims=True)
    total = base[...]
    mixed = jnp.zeros_like(total)
    for i in range(n_exp):
        weight = jnp.sum(jnp.where(ids[...] == i, shares, 0.0), axis=1, keepdims=True)
        both = None
        for j in range(n_dp):
            source = i * n_dp + j

            @pl.when(source != me)
            def _():
                pltpu.make_async_remote_copy(
                    incoming.at[source],
                    incoming.at[source],
                    mix_send.at[0, 0, 0],
                    mix_recv.at[source],
                    device_id=(partner, d, z),
                    device_id_type=MESH,
                ).wait_recv()

            term = incoming[source].astype(F32)
            both = term if both is None else both + term
        mixed = mixed + weight * both
    out[...] = (total + dwa[layers] * mixed).astype(BF16)

    for copy in sends + mixes:
        copy.wait_send()
    for g in range(columns):
        for s in range(pieces):
            for o in range(n_ten):

                @pl.when((o <= z) & has_up)
                def _():
                    hop(g, o, s, True).wait_send()

                @pl.when((o >= z) & has_down)
                def _():
                    hop(g, o, s, False).wait_send()


def solution(mesh):
    n_exp, n_dp, n_ten = (mesh.shape[a] for a in ("expert", "dp", "tensor"))

    def per_device(tokens, ids, route, w_gate, w_up, w_down, past, dwa):
        tok_rows, width = tokens.shape
        units = w_gate.shape[2]
        quarter = w_down.shape[2]
        pieces = 2 if units % 512 == 0 else 1
        piece = units // pieces
        columns, group_rows = n_exp // 2, 2 * n_dp * tok_rows
        blocks = n_exp * n_dp
        any_spec = pl.BlockSpec(memory_space=pl.ANY)
        vmem = pl.BlockSpec(memory_space=pltpu.VMEM)
        smem = pl.BlockSpec(memory_space=pltpu.SMEM)
        dma = pltpu.SemaphoreType.DMA
        return pl.pallas_call(
            functools.partial(kernel, (n_exp, n_dp, n_ten, pieces, tok_rows, quarter)),
            out_shape=jax.ShapeDtypeStruct((tok_rows, quarter), BF16),
            in_specs=[any_spec, vmem, vmem, any_spec, any_spec, any_spec, any_spec, smem],
            out_specs=vmem,
            scratch_shapes=[
                pltpu.VMEM((columns, group_rows, width), BF16),
                pltpu.VMEM((pieces, width, piece), BF16),
                pltpu.VMEM((pieces, width, piece), BF16),
                pltpu.VMEM((n_ten, units, quarter), BF16),
                pltpu.VMEM(past.shape, BF16),
                pltpu.VMEM((columns, n_ten, pieces, group_rows, piece), BF16),
                pltpu.VMEM((columns, group_rows, quarter), F32),
                pltpu.VMEM((columns, group_rows, quarter), BF16),
                pltpu.VMEM((blocks, tok_rows, quarter), BF16),
                pltpu.VMEM((tok_rows, quarter), F32),
                dma,
                dma((pieces,)),
                dma((pieces,)),
                dma((n_ten,)),
                dma,
                dma((columns, n_dp)),
                dma((columns, n_dp)),
                dma((columns, 2 * n_dp)),
                dma((columns, n_ten, pieces, 2)),
                dma((columns, n_ten, pieces)),
                dma((columns, 2, n_dp)),
                dma((blocks,)),
            ],
            compiler_params=pltpu.CompilerParams(
                collective_id=0, has_side_effects=True, vmem_limit_bytes=60 * 1024 * 1024
            ),
        )(tokens, ids, route, w_gate, w_up, w_down, past, dwa)

    return jax.shard_map(
        per_device,
        mesh=mesh,
        in_specs=(
            P(("expert", "dp"), None),
            P(("expert", "dp"), None),
            P(("expert", "dp"), None),
            P("expert", None, ("dp", "tensor")),
            P("expert", None, ("dp", "tensor")),
            P("expert", "dp", "tensor"),
            P(None, ("expert", "dp"), "tensor"),
            P(),
        ),
        out_specs=P(("expert", "dp"), "tensor"),
        check_vma=False,
    )
```

time: 97.3 us -> 45.3 us (0.47)
  blocking collectives: 43.6 us -> 0 us
  Pallas kernels: 0 us -> 40.9 us
  waiting for transfers between devices: 15.8 us -> 0 us
  matrix products: 13.7 us -> 0 us
  between operations: 13.5 us -> 0.01 us
  other arithmetic: 3.56 us -> 0 us
  starting transfers between devices: 3.32 us -> 0 us
    pallas_call x0 -> x1, Pallas kernels: none -> 40.9 us  [per_device(): pl.pallas_call(functools.partial(kernel, (n_exp, n_dp, n_ten, pieces, tok...]
    all_gather x2 -> x0, blocking collectives: 30.7 us -> none  [the longest x1 19.6 us: per_device(): hidden_wide = lax.all_gather(hidden, 'tensor', axis=1, tiled=True)]
    dot_general x5 -> x0, matrix products: 13.7 us -> none  [the longest x1 5.05 us: per_device(): up = jnp.dot(block_rows, w_up, preferred_element_type=jnp.float32)]
    all_to_all x1 -> x0, blocking collectives: 12.9 us -> none  [per_device(): lax.all_to_all(packed, 'expert', split_axis=0, concat_axis=0, tiled=True)]
    reduce_scatter x1 -> x0, waiting for transfers between devices: 11.2 us -> none  [per_device(): lax.psum_scatter(jnp.dot(hidden_wide, w_down, preferred_element_type=jnp....]
    all_to_all x1 -> x0, waiting for transfers between devices: 4.55 us -> none  [per_device(): lax.all_to_all(expert_out.reshape(experts, capacity, quarter), 'expert',...]
    all_to_all x1 -> x0, starting transfers between devices: 3.32 us -> none  [per_device(): lax.all_to_all(expert_out.reshape(experts, capacity, quarter), 'expert',...]
    unnamed x11 -> x3, local copies, waits for them, and re-layouts: 0.82 us -> 4.07 us
  transfers between devices with their start and end apart: 2 -> 0, of which waited for: 2 -> 0; matrix products, arithmetic and copies ran while one was open for 1% -> 0% of each run, Pallas kernels for 0% -> 0%
where the time goes in v1:
time: 45.3 us; the launch traced here: 45 us
  Pallas kernels  40.9 us (90%)
  local copies, waits for them, and re-layouts  4.07 us (9%)
    pallas_call x1, Pallas kernels, per_device(): pl.pallas_call(functools.partial(kernel, (n_exp, n_dp, n_ten, pieces, tok...  40.9 us
    unnamed x3, local copies, waits for them, and re-layouts  4.07 us

profile of v1, /device:TPU:0, one launch (start us, length us, event | category | flops | bytes accessed | tf_op | source)
XLA Modules:
  0.0 45.0 jit_solution(13097593009448158785)
XLA Ops:
  0.0 1.4 %copy.9.ids = s32[16,2]{1,0:T(8,128)} copy(s32[16,2]{0,1:T(2,128)} %param.9) | data formatting | bytes 256 | tf_op args[1]
  1.4 1.3 %copy.10.route = f32[16,2]{1,0:T(8,128)} copy(f32[16,2]{0,1:T(2,128)} %param.10) | data formatting | bytes 256 | tf_op args[2]
  2.7 40.9 %shard_map.82 = bf16[16,1024]{1,0:T(8,128)(2,1)} custom-call(bf16[16,4096]{1,0:T(8,128)(2,1)} %tokens.1, s32[16,2]{1,0:T(8,128)} %copy.9.ids, f32[16,2]{1,0:T(8,128)} %copy.10.route, bf16[1,4096,1024]{2,1,0:T(8,128)(2,1)} %w_gate.1, bf16[1,4096,1024]{2,1,0:T(8,128)(2,1)} %w_up.1, bf16[1,4096,1024]{2,1,0:T(8,128)(2,1)} %w_down.1, bf16[8,16,1024]{2,1,0:T(8,128)(2,1)} %past.1, ...), custom_call_target="tpu_custom_call" | custom-call | tf_op jit(solution)/shard_map/pallas_call | solution.py:352
  43.6 1.4 %copy.12 = bf16[16,1024]{1,0:T(8,128)(2,1)} copy(bf16[16,1024]{1,0:T(8,128)(2,1)} %shard_map.82) | data formatting | bytes 65536

commit v2 on v1

--- a/solution.py
+++ b/solution.py
@@ -43,6 +43,10 @@
     outgoing,
     incoming,
     base,
+    mark,
+    marks,
+    pick,
+    place_back,
     local_sem,
     gate_sem,
     up_sem,
@@ -55,8 +59,10 @@
     z_recv,
     mix_send,
     mix_recv,
+    mark_send,
+    mark_recv,
 ):
-    n_exp, n_dp, n_ten, pieces, tok_rows, quarter = sizes
+    n_exp, n_dp, n_ten, pieces, tok_rows, quarter, capacity = sizes
     columns = n_exp // 2
     in_group = 2 * n_dp
     e, d, z = (lax.axis_index(a) for a in ("expert", "dp", "tensor"))
@@ -80,8 +86,6 @@
                 pltpu.make_async_copy(w_up.at[0, :, part], up_buf.at[s], up_sem.at[s]),
             )
         )
-        for copy in loads[-1]:
-            copy.start()
     past_load = pltpu.make_async_copy(past, past_buf, past_sem)
     past_load.start()
     table = arrival_order(n_ten)
@@ -91,7 +95,7 @@
         for i in range(n_ten):
             o = o + jnp.where(z == i, table[i][j], 0)
         order.append(o)
-    depth = n_ten and down_buf.shape[1]
+    depth = down_buf.shape[1]
     down_loads = []
     for j in range(n_ten):
         o = order[j]
@@ -102,7 +106,15 @@
                 down_sem.at[o],
             )
         )
-        down_loads[-1].start()
+
+    group_rows = in_group * tok_rows
+    expert_row = lax.broadcasted_iota(jnp.int32, (mark.shape[0], tok_rows), 0)
+    named = jnp.zeros(expert_row.shape, F32)
+    for k in range(ids.shape[0]):
+        named = named + jnp.where(ids[k : k + 1, :] == expert_row, 1.0, 0.0)
+    token_at = lax.broadcasted_iota(jnp.int32, (tok_rows, group_rows), 0) + own_place * tok_rows
+    spot = jnp.where(lax.broadcasted_iota(jnp.int32, token_at.shape, 1) == token_at, 1.0, 0.0)
+    mark[...] = jnp.dot(named, spot, preferred_element_type=F32)
 
     barrier = pltpu.get_barrier_semaphore()
     peers = [(i, j) for i in range(n_exp) for j in range(n_dp) if (i, j) != (0, 0)]
@@ -152,13 +164,33 @@
             device_id_type=MESH,
         )
 
-    sends = [to_partner(0, own_place, (0, 0))]
-    sends[0].start()
+    me = e * n_dp + d
+    marks[me] = mark[...]
+    sends = []
+    for i, j in peers:
+        copy = pltpu.make_async_remote_copy(
+            mark,
+            marks.at[me],
+            mark_send.at[i, j],
+            mark_recv.at[me],
+            device_id=(lax.rem(e + i, n_exp), lax.rem(d + j, n_dp), z),
+            device_id_type=MESH,
+        )
+        copy.start()
+        sends.append(copy)
+    sends.append(to_partner(0, own_place, (0, 0)))
+    sends[-1].start()
     hops = [(g, dd) for g in range(columns) for dd in range(n_dp) if (g, dd) != (0, 0)]
     for g, dd in sorted(hops, key=lambda h: (h[0] > 0) + (h[1] > 0)):
         copy = direct(g, dd)
         copy.start()
         sends.append(copy)
+
+    for pair in loads:
+        for copy in pair:
+            copy.start()
+    for copy in down_loads:
+        copy.start()
 
     def wait_tokens(g, place):
         pltpu.make_async_remote_copy(
@@ -194,6 +226,40 @@
             device_id_type=MESH,
         )
 
+    def choose(g):
+        total = jnp.zeros(mark.shape, F32)
+        for c in range(2):
+            for dd in range(n_dp):
+                source = (2 * lax.rem(col + columns - g, columns) + c) * n_dp + dd
+
+                @pl.when(source != me)
+                def _():
+                    pltpu.make_async_remote_copy(
+                        mark,
+                        marks.at[source],
+                        mark_send.at[0, 1],
+                        mark_recv.at[source],
+                        device_id=(partner, d, z),
+                        device_id_type=MESH,
+                    ).wait_recv()
+
+                total = total + marks[source]
+        square = (group_rows, group_rows)
+        before = lax.broadcasted_iota(jnp.int32, square, 0)
+        after = lax.broadcasted_iota(jnp.int32, square, 1)
+        block = lax.div(after, tok_rows)
+        earlier = (before < after) & (lax.div(before, tok_rows) == block)
+        slot = jnp.dot(total, jnp.where(earlier, 1.0, 0.0), preferred_element_type=F32)
+        lane_block = lax.div(lax.broadcasted_iota(jnp.int32, mark.shape, 1), tok_rows)
+        target = jnp.where(total > 0.5, slot + (lane_block * capacity).astype(F32), -1.0)
+        mine = lax.broadcasted_iota(jnp.int32, mark.shape, 0) == e
+        row = jnp.sum(jnp.where(mine, target, 0.0), axis=0, keepdims=True)
+        column = jnp.sum(jnp.where(before == after, row, 0.0), axis=1, keepdims=True)
+        down_slots = lax.broadcasted_iota(jnp.int32, pick.shape[1:], 0).astype(F32)
+        across = lax.broadcasted_iota(jnp.int32, place_back.shape[1:], 1).astype(F32)
+        pick[g] = jnp.where(down_slots == row, 1.0, 0.0).astype(BF16)
+        place_back[g] = jnp.where(across == column, 1.0, 0.0).astype(BF16)
+
     def first_half(g):
         for s in range(pieces):
             if g == 0:
@@ -202,7 +268,8 @@
             rows = rows_in[g]
             gate = jnp.dot(rows, gate_buf[s], preferred_element_type=F32)
             up = jnp.dot(rows, up_buf[s], preferred_element_type=F32)
-            hidden[g, z, s] = (gate / (1.0 + jnp.exp(-gate)) * up).astype(BF16)
+            value = (gate / (1.0 + jnp.exp(-gate)) * up).astype(BF16)
+            hidden[g, z, s] = jnp.dot(pick[g], value, preferred_element_type=F32).astype(BF16)
 
             @pl.when(has_up)
             def _():
@@ -240,10 +307,10 @@
         else:
             acc[g] += total
 
-    me = e * n_dp + d
-
     def give(g):
-        outgoing[g] = acc[g].astype(BF16)
+        outgoing[g] = jnp.dot(
+            place_back[g], acc[g].astype(BF16), preferred_element_type=F32
+        ).astype(BF16)
         copies = []
         for k in range(2):
             for dd in range(n_dp):
@@ -274,12 +341,14 @@
         history = history + dwa[j] * past_buf[j].astype(F32)
     base[...] = history
     own_load.wait()
+    choose(0)
     pass_on(0)
     from_partner(0)
     first_half(0)
     residual = rows_in[0, rows_at(own_place), pl.ds(pl.multiple_of(z * quarter, quarter), quarter)]
     base[...] += dwa[layers] * residual.astype(F32)
     for g in range(1, columns):
+        choose(g)
         pass_on(g)
         from_partner(g)
         first_half(g)
@@ -294,11 +363,14 @@
             if j == n_ten - 1:
                 mixes += give(g)
 
-    shares = route[...] / jnp.sum(route[...], axis=1, keepdims=True)
+    shares = route[...] / jnp.sum(route[...], axis=0, keepdims=True)
+    corner = (tok_rows, tok_rows)
+    diagonal = lax.broadcasted_iota(jnp.int32, corner, 0) == lax.broadcasted_iota(jnp.int32, corner, 1)
     total = base[...]
     mixed = jnp.zeros_like(total)
     for i in range(n_exp):
-        weight = jnp.sum(jnp.where(ids[...] == i, shares, 0.0), axis=1, keepdims=True)
+        weight = jnp.sum(jnp.where(ids[...] == i, shares, 0.0), axis=0, keepdims=True)
+        weight = jnp.sum(jnp.where(diagonal, weight, 0.0), axis=1, keepdims=True)
         both = None
         for j in range(n_dp):
             source = i * n_dp + j
@@ -344,13 +416,16 @@
         pieces = 2 if units % 512 == 0 else 1
         piece = units // pieces
         columns, group_rows = n_exp // 2, 2 * n_dp * tok_rows
+        capacity = min(tok_rows, 3 * ids.shape[1] * tok_rows // (2 * n_exp))
+        packed = 2 * n_dp * capacity
+        named = 8 * pl.cdiv(n_exp, 8)
         blocks = n_exp * n_dp
         any_spec = pl.BlockSpec(memory_space=pl.ANY)
         vmem = pl.BlockSpec(memory_space=pltpu.VMEM)
         smem = pl.BlockSpec(memory_space=pltpu.SMEM)
         dma = pltpu.SemaphoreType.DMA
         return pl.pallas_call(
-            functools.partial(kernel, (n_exp, n_dp, n_ten, pieces, tok_rows, quarter)),
+            functools.partial(kernel, (n_exp, n_dp, n_ten, pieces, tok_rows, quarter, capacity)),
             out_shape=jax.ShapeDtypeStruct((tok_rows, quarter), BF16),
             in_specs=[any_spec, vmem, vmem, any_spec, any_spec, any_spec, any_spec, smem],
             out_specs=vmem,
@@ -360,11 +435,15 @@
                 pltpu.VMEM((pieces, width, piece), BF16),
                 pltpu.VMEM((n_ten, units, quarter), BF16),
                 pltpu.VMEM(past.shape, BF16),
-                pltpu.VMEM((columns, n_ten, pieces, group_rows, piece), BF16),
-                pltpu.VMEM((columns, group_rows, quarter), F32),
+                pltpu.VMEM((columns, n_ten, pieces, packed, piece), BF16),
+                pltpu.VMEM((columns, packed, quarter), F32),
                 pltpu.VMEM((columns, group_rows, quarter), BF16),
                 pltpu.VMEM((blocks, tok_rows, quarter), BF16),
                 pltpu.VMEM((tok_rows, quarter), F32),
+                pltpu.VMEM((named, group_rows), F32),
+                pltpu.VMEM((blocks, named, group_rows), F32),
+                pltpu.VMEM((columns, packed, group_rows), BF16),
+                pltpu.VMEM((columns, group_rows, packed), BF16),
                 dma,
                 dma((pieces,)),
                 dma((pieces,)),
@@ -377,11 +456,13 @@
                 dma((columns, n_ten, pieces)),
                 dma((columns, 2, n_dp)),
                 dma((blocks,)),
+                dma((n_exp, n_dp)),
+                dma((blocks,)),
             ],
             compiler_params=pltpu.CompilerParams(
                 collective_id=0, has_side_effects=True, vmem_limit_bytes=60 * 1024 * 1024
             ),
-        )(tokens, ids, route, w_gate, w_up, w_down, past, dwa)
+        )(tokens, ids.T, route.T, w_gate, w_up, w_down, past, dwa)
 
     return jax.shard_map(
         per_device,

time: 45.3 us -> 39.9 us (0.88)
  local copies, waits for them, and re-layouts: 4.07 us -> 1.38 us
  Pallas kernels: 40.9 us -> 38.4 us
    unnamed x3 -> x1, local copies, waits for them, and re-layouts: 4.07 us -> 1.38 us
    pallas_call x1, Pallas kernels: 40.9 us -> 38.4 us  [per_device(): pl.pallas_call(functools.partial(kernel, (n_exp, n_dp, n_ten, pieces, tok...]
where the time goes in v2:
time: 39.9 us; the launch traced here: 39.8 us
  Pallas kernels  38.4 us (96%)
  local copies, waits for them, and re-layouts  1.38 us (3%)
    pallas_call x1, Pallas kernels, per_device(): pl.pallas_call(functools.partial(kernel, (n_exp, n_dp, n_ten, pieces, tok...  38.4 us
    unnamed x1, local copies, waits for them, and re-layouts  1.38 us

profile of v2, /device:TPU:0, one launch (start us, length us, event | category | flops | bytes accessed | tf_op | source)
XLA Modules:
  0.0 39.8 jit_solution(17330440709579756819)
XLA Ops:
  0.0 38.4 %shard_map.82 = bf16[16,1024]{1,0:T(8,128)(2,1)} custom-call(bf16[16,4096]{1,0:T(8,128)(2,1)} %tokens.1, s32[2,16]{1,0:T(2,128)} %bitcast.2, f32[2,16]{1,0:T(2,128)} %bitcast.3, bf16[1,4096,1024]{2,1,0:T(8,128)(2,1)} %w_gate.1, bf16[1,4096,1024]{2,1,0:T(8,128)(2,1)} %w_up.1, bf16[1,4096,1024]{2,1,0:T(8,128)(2,1)} %w_down.1, bf16[8,16,1024]{2,1,0:T(8,128)(2,1)} %past.1, ...), custom_call_target="tpu_custom_call" | custom-call | tf_op jit(solution)/shard_map/pallas_call | solution.py:427
  38.4 1.4 %copy.10 = bf16[16,1024]{1,0:T(8,128)(2,1)} copy(bf16[16,1024]{1,0:T(8,128)(2,1)} %shard_map.82) | data formatting | bytes 65536

commit v3 on v2

--- a/solution.py
+++ b/solution.py
@@ -202,8 +202,8 @@
             device_id_type=MESH,
         ).wait_recv()
 
-    def pass_on(g):
-        for dd in range(n_dp):
+    def pass_on(g, steps):
+        for dd in steps:
             if (g, dd) == (0, 0):
                 continue
             place = core * n_dp + lax.rem(d + n_dp - dd, n_dp)
@@ -334,22 +334,24 @@
                 copies.append(copy)
         return copies
 
+    own_load.wait()
+    choose(0)
+    pass_on(0, range(n_dp))
+    for g in range(1, columns):
+        pass_on(g, range(1))
+    from_partner(0)
+    first_half(0)
+    residual = rows_in[0, rows_at(own_place), pl.ds(pl.multiple_of(z * quarter, quarter), quarter)]
     past_load.wait()
     layers = past_buf.shape[0]
     history = dwa[0] * past_buf[0].astype(F32)
     for j in range(1, layers):
         history = history + dwa[j] * past_buf[j].astype(F32)
     base[...] = history
-    own_load.wait()
-    choose(0)
-    pass_on(0)
-    from_partner(0)
-    first_half(0)
-    residual = rows_in[0, rows_at(own_place), pl.ds(pl.multiple_of(z * quarter, quarter), quarter)]
     base[...] += dwa[layers] * residual.astype(F32)
     for g in range(1, columns):
         choose(g)
-        pass_on(g)
+        pass_on(g, range(1, n_dp))
         from_partner(g)
         first_half(g)
     mixes = []

time: 39.9 us -> 39.8 us (level)
  no operation moved by 1% of the time
where the time goes in v3:
time: 39.8 us; the launch traced here: 39.6 us
  Pallas kernels  38.2 us (96%)
  local copies, waits for them, and re-layouts  1.38 us (3%)
    pallas_call x1, Pallas kernels, per_device(): pl.pallas_call(functools.partial(kernel, (n_exp, n_dp, n_ten, pieces, tok...  38.2 us
    unnamed x1, local copies, waits for them, and re-layouts  1.38 us

profile of v3, /device:TPU:0, one launch (start us, length us, event | category | flops | bytes accessed | tf_op | source)
XLA Modules:
  0.0 39.6 jit_solution(11216259013837248911)
XLA Ops:
  0.0 38.2 %shard_map.82 = bf16[16,1024]{1,0:T(8,128)(2,1)} custom-call(bf16[16,4096]{1,0:T(8,128)(2,1)} %tokens.1, s32[2,16]{1,0:T(2,128)} %bitcast.2, f32[2,16]{1,0:T(2,128)} %bitcast.3, bf16[1,4096,1024]{2,1,0:T(8,128)(2,1)} %w_gate.1, bf16[1,4096,1024]{2,1,0:T(8,128)(2,1)} %w_up.1, bf16[1,4096,1024]{2,1,0:T(8,128)(2,1)} %w_down.1, bf16[8,16,1024]{2,1,0:T(8,128)(2,1)} %past.1, ...), custom_call_target="tpu_custom_call" | custom-call | tf_op jit(solution)/shard_map/pallas_call | solution.py:429
  38.2 1.4 %copy.10 = bf16[16,1024]{1,0:T(8,128)(2,1)} copy(bf16[16,1024]{1,0:T(8,128)(2,1)} %shard_map.82) | data formatting | bytes 65536
